TPU v7x, 32 devices: a whole 2x2x4 slice. The times are simulated.
32 devices in a mesh: chain: 8 (over y, x, core), cross: 4 (over z).
Axes of the slice: x: 2, y: 2, z: 4, core: 2. Of those that a mesh axis runs over, the one named last changes fastest.
Arguments:
- moments: float32 [20, 512, 1024], P(None, 'cross', 'chain'), as said below
- flags: int32 [512, 1024], P('cross', 'chain'), may hold values from 0 to 2
- shifts: int32 [512, 8], P('cross', 'chain'), may hold values from -48 to 48
- fraction: float32 [512], P('cross'), may hold values from 0.05 to 0.95
Outputs:
- remapped: float32 [20, 512, 1024], P(None, 'cross', 'chain')
- mass_coord: float32 [5, 512, 1024], P(None, 'cross', 'chain')
Inputs may be any that keep to these rules, and one draw needn't show every extreme that they name: zeroth-order moments are positive.
All inputs are finite; a program needn't handle non-finite values.
Results may differ from a plain program's by a relative error of at most 0.000084.
Values sent between devices are 32-bit elements; how exact they have to be, the bound alone decides.
A program may use at most 128 MiB of HBM per device.

v0:
```python
import jax
import jax.numpy as jnp
from jax import lax
from jax.sharding import PartitionSpec as P

VARS = 5
MOMENTS = 4
BLOCK = 128


gauss_nodes = (-0.8611363115940526, -0.3399810435848563, 0.3399810435848563, 0.8611363115940526)
gauss_weights = (0.3478548451374538, 0.6521451548625461, 0.6521451548625461, 0.3478548451374538)


def from_behind(array, axis, by):
    count = lax.axis_size(axis)
    pairs = [(i, i + by) for i in range(count) if 0 <= i + by < count]
    return lax.ppermute(array, axis, pairs)


def legendre_values(point):
    return [
        jnp.ones_like(point),
        point,
        0.5 * (3.0 * point * point - 1.0),
        0.5 * (5.0 * point * point * point - 3.0 * point),
    ]


def interval_matrix(low_end, high_end, offset):
    half = 0.5 * (high_end - low_end)
    middle = 0.5 * (high_end + low_end)
    entries = [[jnp.zeros_like(low_end) for source_order in range(4)] for target_order in range(4)]
    for node, weight in zip(gauss_nodes, gauss_weights):
        point = middle + half * node
        target = legendre_values(point)
        source = legendre_values(point + offset)
        for target_order in range(4):
            for source_order in range(4):
                entries[target_order][source_order] = (
                    entries[target_order][source_order]
                    + weight * half * target[target_order] * source[source_order]
                )
    return jnp.stack(
        [
            jnp.stack(
                [
                    (target_order + 0.5) * entries[target_order][source_order]
                    for source_order in range(4)
                ]
            )
            for target_order in range(4)
        ]
    )


def remap_matrices(fraction):
    first = interval_matrix(-1.0 + 0.0 * fraction, 1.0 - 2.0 * fraction, 2.0 * fraction)
    second = interval_matrix(1.0 - 2.0 * fraction, 1.0 + 0.0 * fraction, 2.0 * fraction - 2.0)
    return (first, second)


def partial_weights(fraction):
    shifted = 2.0 * fraction - 1.0
    square = shifted * shifted
    return jnp.stack(
        [
            fraction,
            fraction * fraction - fraction,
            0.25 * (square * shifted - shifted),
            0.5 * (0.5 * (1.25 * square * square - 1.5 * square) + 0.125),
        ]
    )


def keep_mask(flags):
    order = jnp.arange(4, dtype=jnp.int32)[:, None, None]
    keep = (order == 0) | (order == 1) & (flags[None] <= 1) | (flags[None] == 0)
    return keep.astype(jnp.float32)


def take_window(pencil_rows, start):
    return lax.dynamic_slice_in_dim(pencil_rows, start, BLOCK + 1, 1)


def pencil_windows(pencil_rows, pencil_starts):
    return jax.vmap(take_window, in_axes=(None, 0), out_axes=1)(pencil_rows, pencil_starts)


def shards(moments, flags, shifts, fraction):
    row_count, pencils, cell_count = moments.shape
    expanded = moments.reshape(VARS, MOMENTS, pencils, cell_count)
    limited = (expanded * keep_mask(flags)[None]).reshape(row_count, pencils, cell_count)
    local_sums = jnp.sum(expanded[:, 0], axis=2)
    all_sums = lax.all_gather(local_sums[None], "chain", axis=0, tiled=True)
    my_index = lax.axis_index("chain")
    below_rank = (jnp.arange(all_sums.shape[0], dtype=jnp.int32) < my_index).astype(jnp.float32)
    carried = jnp.einsum("n,nvp->vp", below_rank, all_sums, precision=lax.Precision.HIGHEST)
    grand_sum = lax.psum(jnp.sum(all_sums, axis=(0, 2)), "cross")
    before = from_behind(limited, "chain", 1)
    after = from_behind(limited, "chain", -1)
    extended = jnp.concatenate([before, limited, after], axis=2)
    span = extended.shape[2]
    ext_means = extended.reshape(VARS, MOMENTS, pencils, span)[:, 0]
    positions = jnp.arange(span, dtype=jnp.int32)
    triangle = (positions[:, None] < positions[None, :]).astype(jnp.float32)
    cum_local = jnp.dot(
        ext_means.reshape(VARS * pencils, span), triangle, precision=lax.Precision.HIGHEST
    ).reshape(VARS, pencils, span)
    cum_ext = cum_local - cum_local[:, :, cell_count : cell_count + 1] + carried[:, :, None]
    stacked = jnp.concatenate([extended, cum_ext], axis=0)
    block_count = cell_count // BLOCK
    starts = jnp.arange(block_count, dtype=jnp.int32)[None, :] * BLOCK + shifts + cell_count
    windows = jax.vmap(pencil_windows, in_axes=(1, 0), out_axes=1)(stacked, starts)
    here = windows[:, :, :, :BLOCK].reshape(row_count + VARS, pencils, cell_count)
    beyond = windows[:, :, :, 1:].reshape(row_count + VARS, pencils, cell_count)
    source_cells = here[:row_count].reshape(VARS, MOMENTS, pencils, cell_count)
    next_cells = beyond[:row_count].reshape(VARS, MOMENTS, pencils, cell_count)
    cum_at = here[row_count:]
    first, second = remap_matrices(fraction)
    remapped = jnp.einsum("kmp,vmpc->vkpc", first, source_cells, precision=lax.Precision.HIGHEST)
    remapped = remapped + jnp.einsum(
        "kmp,vmpc->vkpc", second, next_cells, precision=lax.Precision.HIGHEST
    )
    partial_value = jnp.einsum(
        "vmpc,mp->vpc", source_cells, partial_weights(fraction), precision=lax.Precision.HIGHEST
    )
    mean_total = grand_sum / (pencils * lax.axis_size("cross"))
    mass_coord = (cum_at + partial_value) / mean_total[:, None, None]
    return (remapped.reshape(row_count, pencils, cell_count), mass_coord)


def solution(mesh):
    in_specs = (P(None, "cross", "chain"), P("cross", "chain"), P("cross", "chain"), P("cross"))
    out_specs = (P(None, "cross", "chain"), P(None, "cross", "chain"))
    return jax.shard_map(shards, mesh=mesh, in_specs=in_specs, out_specs=out_specs, check_vma=False)
```

profile of v0, /device:TPU:1, one launch (start us, length us, event | category | flops | bytes accessed | tf_op | source)
XLA Modules:
  0.0 153.1 jit_solution(14814393383357451413)
XLA Ops:
  0.6 0.9 broadcast_compare_fusion.1
  1.5 0.1 or_convert_fusion
  1.6 0.0 copy-start
  1.6 0.0 copy-start.1
  1.6 1.4 bitcast_multiply_fusion
  3.1 4.5 %collective-permute-start = (f32[20,128,128]{2,1,0:T(8,128)S(1)}, f32[20,128,128]{2,1,0:T(8,128)S(1)}, u32[]{:S(2)}, u32[]{:S(2)}) collective-permute-start(f32[20,128,128]{2,1,0:T(8,128)S(1)} %bitcast_multiply_fusion), channel_id=1, source_target_pairs={{0,4},{4,8},{8,12},{12,16},{16,20},{20,24},{24,28},{1,5},{5,9},{9,... | collective-permute-start | bytes 3932168 | tf_op jit(solution)/shard_map/ppermute | solution.py:18
  7.6 1.9 %collective-permute-start.1 = (f32[20,128,128]{2,1,0:T(8,128)S(1)}, f32[20,128,128]{2,1,0:T(8,128)}, u32[]{:S(2)}, u32[]{:S(2)}) collective-permute-start(f32[20,128,128]{2,1,0:T(8,128)S(1)} %bitcast_multiply_fusion), channel_id=1, source_target_pairs={{4,0},{8,4},{12,8},{16,12},{20,16},{24,20},{28,24},{5,1},{9,5},{13... | collective-permute-start | bytes 3932168 | tf_op jit(solution)/shard_map/ppermute | solution.py:18
  9.5 1.1 slice_reduce_fusion
  10.7 28.8 %all-gather.1 = f32[8,5,128]{2,1,0:T(8,128)S(1)} all-gather(f32[1,5,128]{2,1,0:T(8,128)S(1)} %bitcast.153), channel_id=2, replica_groups=mesh['chain'=8,'cross'=4] {'chain'}, dimensions={0}, use_global_device_ids=true | all-gather | bytes 23040 | tf_op jit(solution)/shard_map/all_gather | solution.py:95
  39.5 0.0 copy-done
  39.5 0.1 fusion.12
  39.6 0.1 reduce_sum.19
  39.8 9.9 %psum.7 = f32[5]{0:T(128)S(1)} all-reduce(f32[5]{0:T(128)S(1)} %reduce_sum.19), channel_id=1, replica_groups=mesh['chain'=8,'cross'=4] {'cross'}, use_global_device_ids=true, to_apply=%region_2.0 | all-reduce | flops 5 | bytes 40 | tf_op jit(solution)/shard_map/psum | solution.py:99
  49.9 0.2 copy.107
  50.1 0.2 copy.108
  50.3 0.0 copy-done.1
  50.4 0.0 collective-permute-done
  50.4 0.0 collective-permute-done.1
  50.4 1.9 %fusion.7 = f32[5,128,384]{2,1,0:T(8,128)S(1)} fusion(f32[5,4,128,128]{3,2,1,0:T(8,128)} %bitcast.5, f32[5,4,128,128]{3,2,1,0:T(8,128)S(1)} %bitcast.147, f32[5,4,128,128]{3,2,1,0:T(8,128)S(1)} %bitcast.149), kind=kOutput, calls=%fused_computation.14 | convolution fusion | flops 1133101056 | bytes 4915200 | tf_op jit(solution)/shard_map/dot_general | solution.py:107
  52.3 0.2 slice_reduce_fusion.1
  52.5 0.2 subtract_add_fusion
  52.8 4.0 %pad_maximum_fusion = f32[25,128,384]{2,1,0:T(8,128)} fusion(f32[5,128,384]{2,1,0:T(8,128)S(1)} %subtract_add_fusion, f32[20,128,128]{2,1,0:T(8,128)} %collective-permute-done.1, f32[20,128,128]{2,1,0:T(8,128)S(1)} %bitcast_multiply_fusion, f32[20,128,128]{2,1,0:T(8,128)S(1)} %collective-permute-done), kind=kLoop, calls=%fused_computation.4 | loop fusion | flops 3686400 | bytes 9830400 | tf_op jit(solution)/shard_map/concatenate | solution.py:111
  56.7 20.9 %copy.96 = f32[25,128,384]{0,1,2:T(8,128)} copy(f32[25,128,384]{2,1,0:T(8,128)} %pad_maximum_fusion) | data formatting | bytes 9830400 | tf_op jit(solution)/shard_map/concatenate | solution.py:111
  77.7 18.0 %gather_fusion = f32[128,25,129]{1,0,2:T(8,128)} fusion(f32[128,25,384]{1,0,2:T(8,128)} %bitcast.142, s32[128]{0:T(128)S(1)} %or_bitcast_fusion), kind=kCustom, calls=%fused_computation | custom fusion | bytes 3303936 | tf_op jit(solution)/shard_map/vmap(vmap())/gather | solution.py:83
  95.7 10.8 %fusion.115 = (f32[20,128,1,128]{0,1,3,2:T(8,128)}, f32[20,128,1,128]{0,1,3,2:T(8,128)}) fusion(f32[25,128,1,129]{0,1,3,2:T(8,128)} %bitcast.143), kind=kLoop, calls=%fused_computation.244 | loop fusion | bytes 5242880 | tf_op jit(solution)/shard_map/slice | solution.py:118
  106.5 7.0 %copy.97 = f32[20,128,1,128]{3,1,0,2:T(8,128)S(1)} copy(f32[20,128,1,128]{0,1,3,2:T(8,128)} %get-tuple-element.25) | data formatting | bytes 2621440 | tf_op jit(solution)/shard_map/slice | solution.py:117
  113.5 0.1 multiply_reduce_fusion
  113.6 7.5 %copy.114 = f32[128,5,128]{1,0,2:T(8,128)} copy(f32[128,5,128]{2,0,1:T(8,128)S(1)} %multiply_reduce_fusion) | data formatting | bytes 655360 | tf_op jit(solution)/shard_map/vmpc,mp->vpc/dot_general | solution.py:125
  121.2 9.5 %fusion.1 = f32[5,128,128]{0,1,2:T(8,128)} fusion(f32[25,128,1,129]{0,1,3,2:T(8,128)} %bitcast.144, f32[128,5,128]{1,0,2:T(8,128)} %copy.114, f32[5]{0:T(128)S(1)} %broadcast_multiply_fusion), kind=kLoop, calls=%fused_computation.3 | loop fusion | flops 163840 | bytes 983060 | tf_op jit(solution)/shard_map/div | solution.py:129
  130.7 7.2 %copy.104 = f32[5,128,128]{2,1,0:T(8,128)} copy(f32[5,128,128]{0,1,2:T(8,128)} %fusion.1) | data formatting | bytes 655360
  137.9 6.8 %copy.100 = f32[20,128,1,128]{3,1,0,2:T(8,128)S(1)} copy(f32[20,128,1,128]{0,1,3,2:T(8,128)} %get-tuple-element.24) | data formatting | bytes 2621440 | tf_op jit(solution)/shard_map/slice | solution.py:118
  144.7 3.5 %fusion.4 = f32[128,5,128,4]{2,3,1,0:T(4,128)S(1)} fusion(f32[4,4,128,1]{1,0,3,2:T(4,128)S(1)} %copy.107, f32[5,4,128,128]{3,2,1,0:T(8,128)S(1)} %bitcast.146), kind=kOutput, calls=%fused_computation.10 | convolution fusion | flops 15728640 | bytes 2629632 | tf_op jit(solution)/shard_map/kmp,vmpc->vkpc/dot_general | solution.py:121
  148.2 3.6 %fusion.2 = f32[5,4,128,128]{3,1,0,2:T(4,128)S(1)} fusion(f32[128,5,128,4]{2,3,1,0:T(4,128)S(1)} %fusion.4, f32[4,4,128,1]{1,0,3,2:T(4,128)S(1)} %copy.108, f32[5,4,128,128]{3,2,1,0:T(8,128)S(1)} %bitcast.148), kind=kOutput, calls=%fused_computation.6 | convolution fusion | flops 16056320 | bytes 3940352 | tf_op jit(solution)/shard_map/kmp,vmpc->vkpc/dot_general | solution.py:122
  151.9 1.2 copy.103
  (19 shorter events, 0.2 us)
Async XLA Ops:
  1.6 37.9 %copy-start = (f32[128]{0:T(128)S(1)}, f32[128]{0:T(128)}, u32[]{:S(2)}) copy-start(f32[128]{0:T(128)} %param.7) | copy-start | bytes 1540
  1.6 48.7 %copy-start.1 = (s32[128,1]{0,1:T(1,128)S(1)}, s32[128,1]{0,1:T(1,128)}, u32[]{:S(2)}) copy-start(s32[128,1]{0,1:T(1,128)} %param.6) | copy-start | bytes 1540
  3.1 47.3 %collective-permute-start = (f32[20,128,128]{2,1,0:T(8,128)S(1)}, f32[20,128,128]{2,1,0:T(8,128)S(1)}, u32[]{:S(2)}, u32[]{:S(2)}) collective-permute-start(f32[20,128,128]{2,1,0:T(8,128)S(1)} %bitcast_multiply_fusion), channel_id=1, source_target_pairs={{0,4},{4,8},{8,12},{12,16},{16,20},{20,24},{24,28},{1,5},{5,9},{9,... | collective-permute-start | bytes 3932168 | tf_op jit(solution)/shard_map/ppermute | solution.py:18
  7.6 42.8 %collective-permute-start.1 = (f32[20,128,128]{2,1,0:T(8,128)S(1)}, f32[20,128,128]{2,1,0:T(8,128)}, u32[]{:S(2)}, u32[]{:S(2)}) collective-permute-start(f32[20,128,128]{2,1,0:T(8,128)S(1)} %bitcast_multiply_fusion), channel_id=1, source_target_pairs={{4,0},{8,4},{12,8},{16,12},{20,16},{24,20},{28,24},{5,1},{9,5},{13... | collective-permute-start | bytes 3932168 | tf_op jit(solution)/shard_map/ppermute | solution.py:18
where the time goes:
time: 156 us; the launch traced here: 153 us
  local copies, waits for them, and re-layouts  80.1 us (51%)
  blocking collectives  38.8 us (25%)
  other arithmetic  17.7 us (11%)
  matrix products  9.18 us (6%)
  starting transfers between devices  6.42 us (4%)
    all_gather x1, blocking collectives, shards(): all_sums = lax.all_gather(local_sums[None], 'chain', axis=0, tiled=True)  28.8 us
    concatenate x1, local copies, waits for them, and re-layouts, shards(): stacked = jnp.concatenate([extended, cum_ext], axis=0)  20.9 us
    gather x1, local copies, waits for them, and re-layouts, take_window(): return lax.dynamic_slice_in_dim(pencil_rows, start, BLOCK + 1, 1)  18 us
    slice x2, local copies, waits for them, and re-layouts, shards(): next_cells = beyond[:row_count].reshape(VARS, MOMENTS, pencils, cell_count)  17.6 us
    psum x1, blocking collectives, shards(): grand_sum = lax.psum(jnp.sum(all_sums, axis=(0, 2)), 'cross')  9.95 us
    div x1, other arithmetic, shards(): mass_coord = (cum_at + partial_value) / mean_total[:, None, None]  9.48 us
    dot_general x1, local copies, waits for them, and re-layouts, shards(): jnp.einsum('vmpc,mp->vpc', source_cells, partial_weights(fraction), preci...  7.54 us
    unnamed x6, local copies, waits for them, and re-layouts  7.26 us
  transfers between devices with their start and end apart: 2, of which 0 were waited for; matrix products, arithmetic and copies ran while one was open for 1% of the time, Pallas kernels for 0%

commit v1 on v0

v1 whole, which is shorter than its diff:
```python
import functools

import jax
import jax.numpy as jnp
from jax import lax
from jax.experimental import pallas as pl
from jax.experimental.pallas import tpu as pltpu
from jax.sharding import PartitionSpec as P

VARS = 5
MOMENTS = 4
BLOCK = 128
SHIFT_MAX = 48
ROWS = VARS * MOMENTS
STRIDE = SHIFT_MAX + 1
CHUNKS = -(-ROWS * STRIDE // BLOCK)
GROUP = 8
COEFS = 2 * MOMENTS * MOMENTS + MOMENTS
MESH = pl.DeviceIdType.MESH
HIGHEST = lax.Precision.HIGHEST

gauss_nodes = (-0.8611363115940526, -0.3399810435848563, 0.3399810435848563, 0.8611363115940526)
gauss_weights = (0.3478548451374538, 0.6521451548625461, 0.6521451548625461, 0.3478548451374538)


def segments(first, length):
    held = [[] for _ in range(CHUNKS)]
    for row in range(ROWS):
        start = first + STRIDE * row
        chunk, lane = divmod(start, BLOCK)
        held[chunk % CHUNKS].append((lane, row))
        if lane + length > BLOCK:
            held[(chunk + 1) % CHUNKS].append((0, row))
    return [sorted(chunk) for chunk in held]


AFTER_FIRST, AFTER_LENGTH = SHIFT_MAX, SHIFT_MAX + 1
BEFORE_FIRST, BEFORE_LENGTH = 0, SHIFT_MAX
AFTER = segments(AFTER_FIRST, AFTER_LENGTH)
BEFORE = segments(BEFORE_FIRST, BEFORE_LENGTH)


def places(row, first, length):
    chunk, lane = divmod(first + STRIDE * row, BLOCK)
    chunks = [chunk % CHUNKS]
    if lane + length > BLOCK:
        chunks.append((chunk + 1) % CHUNKS)
    return chunks, lane


def last_chunk(var):
    need = [0]
    for row in range(MOMENTS * var, MOMENTS * (var + 1)):
        need += places(row, AFTER_FIRST, AFTER_LENGTH)[0]
        need += places(row, BEFORE_FIRST, BEFORE_LENGTH)[0]
    return max(need)


def legendre_values(point):
    return [
        jnp.ones_like(point),
        point,
        0.5 * (3.0 * point * point - 1.0),
        0.5 * (5.0 * point * point * point - 3.0 * point),
    ]


def interval_matrix(low_end, high_end, offset):
    half = 0.5 * (high_end - low_end)
    middle = 0.5 * (high_end + low_end)
    entries = [[jnp.zeros_like(low_end) for _ in range(4)] for _ in range(4)]
    for node, weight in zip(gauss_nodes, gauss_weights):
        point = middle + half * node
        target = legendre_values(point)
        source = legendre_values(point + offset)
        for k in range(4):
            scaled = weight * half * target[k]
            for m in range(4):
                entries[k][m] = entries[k][m] + scaled * source[m]
    return [(k + 0.5) * entries[k][m] for k in range(4) for m in range(4)]


def partial_weights(fraction):
    shifted = 2.0 * fraction - 1.0
    square = shifted * shifted
    return [
        fraction,
        fraction * fraction - fraction,
        0.25 * (square * shifted - shifted),
        0.5 * (0.5 * (1.25 * square * square - 1.5 * square) + 0.125),
    ]


def kernel(
    chain, cross,
    moments, flags, shifts, fraction,
    remapped, mass,
    to_left, to_right, from_left, from_right,
    sums, parts, raw, coef, carried, shift_of, mean_of, window,
    left_send, left_recv, right_send, right_recv,
    sum_send, sum_recv, part_send, part_recv,
):
    pencils = moments.shape[1]
    groups = pencils // GROUP
    me = lax.axis_index("chain")
    plane = lax.axis_index("cross")

    barrier = pltpu.get_barrier_semaphore()
    for step in range(1, chain):
        peer = lax.rem(me + step, chain)
        pl.semaphore_signal(barrier, inc=1, device_id={"chain": peer}, device_id_type=MESH)
    for step in range(1, cross):
        peer = lax.rem(plane + step, cross)
        pl.semaphore_signal(barrier, inc=1, device_id={"cross": peer}, device_id_type=MESH)

    row_id = lax.broadcasted_iota(jnp.int32, (8, BLOCK), 0)
    total = jnp.zeros((8, pencils), jnp.float32)
    for var in range(VARS):
        pick = (row_id == var).astype(jnp.float32)
        total = total + lax.dot_general(
            pick, moments[MOMENTS * var], (((1,), (1,)), ((), ())),
            precision=HIGHEST, preferred_element_type=jnp.float32,
        )
    sums[me] = total

    lane = lax.broadcasted_iota(jnp.int32, (GROUP, BLOCK), 1)

    def limited_row(row, rows, keep_linear, keep_full):
        value = moments[row, rows, :]
        order = row % MOMENTS
        if order == 1:
            value = jnp.where(keep_linear, value, 0.0)
        elif order > 1:
            value = jnp.where(keep_full, value, 0.0)
        return value

    def pack(group, carry):
        rows = pl.ds(pl.multiple_of(group * GROUP, GROUP), GROUP)
        flag = flags[rows, :]
        keep_linear, keep_full = flag <= 1, flag == 0
        rolled = [
            pltpu.roll(
                limited_row(row, rows, keep_linear, keep_full),
                (STRIDE * row + SHIFT_MAX) % BLOCK, 1,
            )
            for row in range(ROWS)
        ]
        for chunk in range(CHUNKS):
            for held, target in ((AFTER, to_left), (BEFORE, to_right)):
                value = rolled[held[chunk][0][1]]
                for start, row in held[chunk][1:]:
                    value = jnp.where(lane >= start, rolled[row], value)
                target[chunk, rows, :] = value
        return carry

    lax.fori_loop(0, groups, pack, 0)

    pl.semaphore_wait(barrier, chain - 1 + cross - 1)

    sum_copies = []
    for step in range(1, chain):
        copy = pltpu.make_async_remote_copy(
            src_ref=sums.at[me], dst_ref=sums.at[me],
            send_sem=sum_send.at[step], recv_sem=sum_recv.at[step],
            device_id={"chain": lax.rem(me + step, chain)}, device_id_type=MESH,
        )
        copy.start()
        sum_copies.append(copy)

    def leftward(chunk):
        return pltpu.make_async_remote_copy(
            src_ref=to_left.at[chunk], dst_ref=from_right.at[chunk],
            send_sem=left_send.at[chunk], recv_sem=left_recv.at[chunk],
            device_id={"chain": lax.rem(me + chain - 1, chain)}, device_id_type=MESH,
        )

    def rightward(chunk):
        return pltpu.make_async_remote_copy(
            src_ref=to_right.at[chunk], dst_ref=from_left.at[chunk],
            send_sem=right_send.at[chunk], recv_sem=right_recv.at[chunk],
            device_id={"chain": lax.rem(me + 1, chain)}, device_id_type=MESH,
        )

    has_left, has_right = me > 0, me < chain - 1

    @pl.when(has_left)
    def _():
        for chunk in range(CHUNKS):
            leftward(chunk).start()

    @pl.when(has_right)
    def _():
        for chunk in range(CHUNKS):
            rightward(chunk).start()

    @pl.when(me == 0)
    def _():
        from_left[...] = jnp.zeros_like(from_left)

    @pl.when(me == chain - 1)
    def _():
        from_right[...] = jnp.zeros_like(from_right)

    f = fraction[...]
    first = interval_matrix(-1.0 + 0.0 * f, 1.0 - 2.0 * f, 2.0 * f)
    second = interval_matrix(1.0 - 2.0 * f, 1.0 + 0.0 * f, 2.0 * f - 2.0)
    raw[...] = jnp.zeros_like(raw)
    columns = first + second + partial_weights(f) + [shifts[...].astype(jnp.float32)]
    for index, value in enumerate(columns):
        raw[index : index + 1, :] = value
    turned = jnp.transpose(raw[...])
    for index in range(COEFS):
        coef[index] = jnp.broadcast_to(turned[:, index : index + 1], (pencils, BLOCK))
    shift_of[...] = jnp.broadcast_to(turned[:, COEFS : COEFS + 1], (pencils, BLOCK)).astype(jnp.int32)

    for copy in sum_copies:
        copy.wait_recv()
    before = jnp.zeros((8, pencils), jnp.float32)
    whole = jnp.zeros((8, pencils), jnp.float32)
    for index in range(chain):
        value = sums[index]
        before = before + jnp.where(index < me, value, 0.0)
        whole = whole + value
    parts[plane] = jnp.broadcast_to(jnp.sum(whole, axis=1, keepdims=True), (8, BLOCK))
    part_copies = []
    for step in range(1, cross):
        copy = pltpu.make_async_remote_copy(
            src_ref=parts.at[plane], dst_ref=parts.at[plane],
            send_sem=part_send.at[step], recv_sem=part_recv.at[step],
            device_id={"cross": lax.rem(plane + step, cross)}, device_id_type=MESH,
        )
        copy.start()
        part_copies.append(copy)
    raw[0:8, :] = before
    turned = jnp.transpose(raw[...])
    for var in range(VARS):
        carried[var] = jnp.broadcast_to(turned[:, var : var + 1], (pencils, BLOCK))
    for copy in part_copies:
        copy.wait_recv()
    grand = parts[0]
    for index in range(1, cross):
        grand = grand + parts[index]
    mean_of[...] = grand / float(pencils * cross)

    source_cell = lax.broadcasted_iota(jnp.int32, (2 * BLOCK, BLOCK), 0)
    target_cell = lax.broadcasted_iota(jnp.int32, (2 * BLOCK, BLOCK), 1)
    triangle = jnp.where((source_cell < target_cell) | (source_cell >= BLOCK), 1.0, 0.0)

    def halo_row(row, rows, ahead):
        values = []
        for ref, first_lane, length in (
            (from_right, AFTER_FIRST, AFTER_LENGTH),
            (from_left, BEFORE_FIRST, BEFORE_LENGTH),
        ):
            chunks, start = places(row, first_lane, length)
            value = ref[chunks[0], rows, :]
            if len(chunks) > 1:
                value = jnp.where(lane >= start, value, ref[chunks[1], rows, :])
            values.append(value)
        value = jnp.where(ahead, values[0], values[1])
        return pltpu.roll(value, (-(STRIDE * row + SHIFT_MAX)) % BLOCK, 1)

    ready = 0
    for var in range(VARS):
        needed = last_chunk(var) + 1
        if needed > ready:
            low, ready = ready, needed

            @pl.when(has_right)
            def _(low=low, high=needed):
                for chunk in range(low, high):
                    leftward(chunk).wait_recv()

            @pl.when(has_left)
            def _(low=low, high=needed):
                for chunk in range(low, high):
                    rightward(chunk).wait_recv()

        def remap(group, carry, var=var):
            rows = pl.ds(pl.multiple_of(group * GROUP, GROUP), GROUP)
            flag = flags[rows, :]
            keep_linear, keep_full = flag <= 1, flag == 0
            shift = shift_of[rows, :]
            ahead = shift >= 0
            turn = shift & (BLOCK - 1)
            outside = jnp.where(ahead, lane - turn, turn - 1 - lane) < 0
            outside_next = jnp.where(ahead, lane - turn - 1, turn - lane) < 0
            at = (lane + turn) & (BLOCK - 1)
            at_next = (lane + turn + 1) & (BLOCK - 1)
            here, beyond = [], []
            for order in range(MOMENTS):
                row = MOMENTS * var + order
                own = limited_row(row, rows, keep_linear, keep_full)
                halo = halo_row(row, rows, ahead)
                here.append(
                    jnp.take_along_axis(
                        jnp.where(outside, halo, own), at, axis=1, mode="promise_in_bounds"
                    )
                )
                beyond.append(
                    jnp.take_along_axis(
                        jnp.where(outside_next, halo, own), at_next, axis=1, mode="promise_in_bounds"
                    )
                )
                if order == 0:
                    gap = jnp.where(outside, jnp.where(ahead, own, -halo), 0.0)
            window[rows, 0:BLOCK] = here[0]
            window[rows, BLOCK : 2 * BLOCK] = gap
            for k in range(MOMENTS):
                value = None
                for m in range(MOMENTS):
                    term = coef[MOMENTS * k + m, rows, :] * here[m]
                    value = term if value is None else value + term
                    value = value + coef[MOMENTS * (MOMENTS + k) + m, rows, :] * beyond[m]
                remapped[MOMENTS * var + k, rows, :] = value
            value = coef[2 * MOMENTS * MOMENTS, rows, :] * here[0]
            for m in range(1, MOMENTS):
                value = value + coef[2 * MOMENTS * MOMENTS + m, rows, :] * here[m]
            mass[var, rows, :] = value + carried[var, rows, :]
            return carry

        lax.fori_loop(0, groups, remap, 0)
        summed = jnp.dot(
            window[...], triangle, precision=HIGHEST, preferred_element_type=jnp.float32
        )
        mass[var] = (summed + mass[var]) / mean_of[var : var + 1, :]

    for copy in sum_copies + part_copies:
        copy.wait_send()

    @pl.when(has_left)
    def _():
        for chunk in range(CHUNKS):
            leftward(chunk).wait_send()

    @pl.when(has_right)
    def _():
        for chunk in range(CHUNKS):
            rightward(chunk).wait_send()


def solution(mesh):
    chain, cross = mesh.shape["chain"], mesh.shape["cross"]

    def shards(moments, flags, shifts, fraction):
        row_count, pencils, cells = moments.shape
        assert row_count == ROWS and cells == BLOCK and pencils == BLOCK
        chunk = pltpu.VMEM((CHUNKS, pencils, BLOCK), jnp.float32)
        dma = pltpu.SemaphoreType.DMA
        return pl.pallas_call(
            functools.partial(kernel, chain, cross),
            out_shape=(
                jax.ShapeDtypeStruct(moments.shape, jnp.float32),
                jax.ShapeDtypeStruct((VARS, pencils, cells), jnp.float32),
            ),
            in_specs=[pl.BlockSpec(memory_space=pltpu.VMEM)] * 4,
            out_specs=(pl.BlockSpec(memory_space=pltpu.VMEM),) * 2,
            scratch_shapes=[
                chunk, chunk, chunk, chunk,
                pltpu.VMEM((chain, 8, pencils), jnp.float32),
                pltpu.VMEM((cross, 8, BLOCK), jnp.float32),
                pltpu.VMEM((BLOCK, pencils), jnp.float32),
                pltpu.VMEM((COEFS, pencils, BLOCK), jnp.float32),
                pltpu.VMEM((VARS, pencils, BLOCK), jnp.float32),
                pltpu.VMEM((pencils, BLOCK), jnp.int32),
                pltpu.VMEM((8, BLOCK), jnp.float32),
                pltpu.VMEM((pencils, 2 * BLOCK), jnp.float32),
                dma((CHUNKS,)), dma((CHUNKS,)), dma((CHUNKS,)), dma((CHUNKS,)),
                dma((chain,)), dma((chain,)), dma((cross,)), dma((cross,)),
            ],
            compiler_params=pltpu.CompilerParams(
                collective_id=0, has_side_effects=True, vmem_limit_bytes=48 << 20
            ),
        )(moments, flags, shifts.T, fraction.reshape(1, pencils))

    in_specs = (P(None, "cross", "chain"), P("cross", "chain"), P("cross", "chain"), P("cross"))
    out_specs = (P(None, "cross", "chain"), P(None, "cross", "chain"))
    return jax.shard_map(shards, mesh=mesh, in_specs=in_specs, out_specs=out_specs, check_vma=False)
```

time: 156 us -> 34.2 us (0.22)
  the two profiles are of different devices: /device:TPU:1 before, /device:TPU:0 now
where the time goes in v1:
time: 34.2 us; the launch traced here: 34 us
  Pallas kernels  28.1 us (82%)
  local copies, waits for them, and re-layouts  5.24 us (15%)
  between operations  0.65 us (2%)
    pallas_call x1, Pallas kernels, shards(): pl.pallas_call(functools.partial(kernel, chain, cross), out_shape=(jax.Sh...  28.1 us
    unnamed x10, local copies, waits for them, and re-layouts  5.24 us

profile of v1, /device:TPU:0, one launch (start us, length us, event | category | flops | bytes accessed | tf_op | source)
XLA Modules:
  0.0 34.0 jit_solution(12869140786851690274)
XLA Ops:
  0.6 0.0 copy-start
  0.6 1.3 %copy-done = f32[20,128,128]{2,1,0:T(8,128)S(1)} copy-done((f32[20,128,128]{2,1,0:T(8,128)S(1)}, f32[20,128,128]{2,1,0:T(8,128)}, u32[]{:S(2)}) %copy-start) | copy-done | bytes 1310744
  1.9 0.0 copy-start.1
  1.9 0.8 %copy-done.1 = s32[128,128]{1,0:T(8,128)S(1)} copy-done((s32[128,128]{1,0:T(8,128)S(1)}, s32[128,128]{1,0:T(8,128)}, u32[]{:S(2)}) %copy-start.1) | copy-done | bytes 65560
  2.8 0.0 copy-start.2
  2.8 0.7 %copy-done.2 = s32[128,1]{0,1:T(1,128)S(1)} copy-done((s32[128,1]{0,1:T(1,128)S(1)}, s32[128,1]{0,1:T(1,128)}, u32[]{:S(2)}) %copy-start.2) | copy-done | bytes 536
  3.4 0.0 copy-start.3
  3.4 0.7 %copy-done.3 = f32[128]{0:T(128)S(1)} copy-done((f32[128]{0:T(128)S(1)}, f32[128]{0:T(128)}, u32[]{:S(2)}) %copy-start.3) | copy-done | bytes 536
  4.1 28.1 %shard_map.59 = (f32[20,128,128]{2,1,0:T(8,128)S(1)}, f32[5,128,128]{2,1,0:T(8,128)S(1)}) custom-call(f32[20,128,128]{2,1,0:T(8,128)S(1)} %copy-done, s32[128,128]{1,0:T(8,128)S(1)} %copy-done.1, s32[1,128]{1,0:T(1,128)S(1)} %bitcast.2, f32[1,128]{1,0:T(1,128)S(1)} %bitcast.3), custom_call_target="tpu_custom_call" | custom-call | tf_op jit(solution)/shard_map/pallas_call | solution.py:350
  32.2 1.1 %copy.8 = f32[20,128,128]{2,1,0:T(8,128)} copy(f32[20,128,128]{2,1,0:T(8,128)S(1)} %get-tuple-element.4) | data formatting | bytes 2621440
  33.3 0.7 %copy.9 = f32[5,128,128]{2,1,0:T(8,128)} copy(f32[5,128,128]{2,1,0:T(8,128)S(1)} %get-tuple-element.5) | data formatting | bytes 655360
Async XLA Ops:
  0.6 1.3 %copy-start = (f32[20,128,128]{2,1,0:T(8,128)S(1)}, f32[20,128,128]{2,1,0:T(8,128)}, u32[]{:S(2)}) copy-start(f32[20,128,128]{2,1,0:T(8,128)} %moments.1) | copy-start | bytes 3932164
  1.9 0.8 %copy-start.1 = (s32[128,128]{1,0:T(8,128)S(1)}, s32[128,128]{1,0:T(8,128)}, u32[]{:S(2)}) copy-start(s32[128,128]{1,0:T(8,128)} %flags.1) | copy-start | bytes 196612
  2.8 0.7 %copy-start.2 = (s32[128,1]{0,1:T(1,128)S(1)}, s32[128,1]{0,1:T(1,128)}, u32[]{:S(2)}) copy-start(s32[128,1]{0,1:T(1,128)} %param.6) | copy-start | bytes 1540
  3.4 0.7 %copy-start.3 = (f32[128]{0:T(128)S(1)}, f32[128]{0:T(128)}, u32[]{:S(2)}) copy-start(f32[128]{0:T(128)} %param.7) | copy-start | bytes 1540

commit v2 on v1

--- a/solution.py
+++ b/solution.py
@@ -14,7 +14,9 @@
 ROWS = VARS * MOMENTS
 STRIDE = SHIFT_MAX + 1
 CHUNKS = -(-ROWS * STRIDE // BLOCK)
-GROUP = 8
+GROUP = 64
+SEND_SUMS = 2
+SUMS_AT = 3
 COEFS = 2 * MOMENTS * MOMENTS + MOMENTS
 MESH = pl.DeviceIdType.MESH
 HIGHEST = lax.Precision.HIGHEST
@@ -93,17 +95,27 @@
 
 def kernel(
     chain, cross,
+    moments_in, flags_in, shifts_in, fraction_in,
+    remapped, mass,
     moments, flags, shifts, fraction,
-    remapped, mass,
     to_left, to_right, from_left, from_right,
     sums, parts, raw, coef, carried, shift_of, mean_of, window,
     left_send, left_recv, right_send, right_recv,
-    sum_send, sum_recv, part_send, part_recv,
+    sum_send, sum_recv, part_send, part_recv, input_sem,
 ):
     pencils = moments.shape[1]
     groups = pencils // GROUP
     me = lax.axis_index("chain")
     plane = lax.axis_index("cross")
+
+    inputs = [
+        pltpu.make_async_copy(source, target, input_sem.at[index])
+        for index, (source, target) in enumerate(
+            ((moments_in, moments), (flags_in, flags), (shifts_in, shifts), (fraction_in, fraction))
+        )
+    ]
+    for copy in inputs:
+        copy.start()
 
     barrier = pltpu.get_barrier_semaphore()
     for step in range(1, chain):
@@ -113,15 +125,8 @@
         peer = lax.rem(plane + step, cross)
         pl.semaphore_signal(barrier, inc=1, device_id={"cross": peer}, device_id_type=MESH)
 
-    row_id = lax.broadcasted_iota(jnp.int32, (8, BLOCK), 0)
-    total = jnp.zeros((8, pencils), jnp.float32)
-    for var in range(VARS):
-        pick = (row_id == var).astype(jnp.float32)
-        total = total + lax.dot_general(
-            pick, moments[MOMENTS * var], (((1,), (1,)), ((), ())),
-            precision=HIGHEST, preferred_element_type=jnp.float32,
-        )
-    sums[me] = total
+    for copy in inputs:
+        copy.wait()
 
     lane = lax.broadcasted_iota(jnp.int32, (GROUP, BLOCK), 1)
 
@@ -134,64 +139,80 @@
             value = jnp.where(keep_full, value, 0.0)
         return value
 
-    def pack(group, carry):
-        rows = pl.ds(pl.multiple_of(group * GROUP, GROUP), GROUP)
-        flag = flags[rows, :]
-        keep_linear, keep_full = flag <= 1, flag == 0
-        rolled = [
-            pltpu.roll(
-                limited_row(row, rows, keep_linear, keep_full),
-                (STRIDE * row + SHIFT_MAX) % BLOCK, 1,
+    def leftward(chunk):
+        return pltpu.make_async_remote_copy(
+            src_ref=to_left.at[chunk], dst_ref=from_right.at[chunk],
+            send_sem=left_send.at[chunk], recv_sem=left_recv.at[chunk],
+            device_id={"chain": lax.rem(me + chain - 1, chain)}, device_id_type=MESH,
+        )
+
+    def rightward(chunk):
+        return pltpu.make_async_remote_copy(
+            src_ref=to_right.at[chunk], dst_ref=from_left.at[chunk],
+            send_sem=right_send.at[chunk], recv_sem=right_recv.at[chunk],
+            device_id={"chain": lax.rem(me + 1, chain)}, device_id_type=MESH,
+        )
+
+    has_left, has_right = me > 0, me < chain - 1
+
+    sum_copies = [
+        pltpu.make_async_remote_copy(
+            src_ref=sums.at[me], dst_ref=sums.at[me],
+            send_sem=sum_send.at[step], recv_sem=sum_recv.at[step],
+            device_id={"chain": lax.rem(me + step, chain)}, device_id_type=MESH,
+        )
+        for step in range(1, chain)
+    ]
+
+    def send_sums():
+        row_id = lax.broadcasted_iota(jnp.int32, (8, BLOCK), 0)
+        total = jnp.zeros((8, pencils), jnp.float32)
+        for var in range(VARS):
+            pick = (row_id == var).astype(jnp.float32)
+            total = total + lax.dot_general(
+                pick, moments[MOMENTS * var], (((1,), (1,)), ((), ())),
+                precision=HIGHEST, preferred_element_type=jnp.float32,
             )
-            for row in range(ROWS)
-        ]
-        for chunk in range(CHUNKS):
+        sums[me] = total
+        for copy in sum_copies:
+            copy.start()
+
+    def pack(chunk):
+        def body(group, carry):
+            rows = pl.ds(pl.multiple_of(group * GROUP, GROUP), GROUP)
+            flag = flags[rows, :]
+            keep_linear, keep_full = flag <= 1, flag == 0
+            rolled = {
+                row: pltpu.roll(
+                    limited_row(row, rows, keep_linear, keep_full),
+                    (STRIDE * row + SHIFT_MAX) % BLOCK, 1,
+                )
+                for row in sorted({row for held in (AFTER, BEFORE) for _, row in held[chunk]})
+            }
             for held, target in ((AFTER, to_left), (BEFORE, to_right)):
                 value = rolled[held[chunk][0][1]]
                 for start, row in held[chunk][1:]:
                     value = jnp.where(lane >= start, rolled[row], value)
                 target[chunk, rows, :] = value
-        return carry
-
-    lax.fori_loop(0, groups, pack, 0)
-
-    pl.semaphore_wait(barrier, chain - 1 + cross - 1)
-
-    sum_copies = []
-    for step in range(1, chain):
-        copy = pltpu.make_async_remote_copy(
-            src_ref=sums.at[me], dst_ref=sums.at[me],
-            send_sem=sum_send.at[step], recv_sem=sum_recv.at[step],
-            device_id={"chain": lax.rem(me + step, chain)}, device_id_type=MESH,
-        )
-        copy.start()
-        sum_copies.append(copy)
-
-    def leftward(chunk):
-        return pltpu.make_async_remote_copy(
-            src_ref=to_left.at[chunk], dst_ref=from_right.at[chunk],
-            send_sem=left_send.at[chunk], recv_sem=left_recv.at[chunk],
-            device_id={"chain": lax.rem(me + chain - 1, chain)}, device_id_type=MESH,
-        )
-
-    def rightward(chunk):
-        return pltpu.make_async_remote_copy(
-            src_ref=to_right.at[chunk], dst_ref=from_left.at[chunk],
-            send_sem=right_send.at[chunk], recv_sem=right_recv.at[chunk],
-            device_id={"chain": lax.rem(me + 1, chain)}, device_id_type=MESH,
-        )
-
-    has_left, has_right = me > 0, me < chain - 1
-
-    @pl.when(has_left)
-    def _():
-        for chunk in range(CHUNKS):
+            return carry
+
+        lax.fori_loop(0, groups, body, 0)
+
+    for chunk in range(CHUNKS):
+        pack(chunk)
+        if chunk == 0:
+            pl.semaphore_wait(barrier, chain - 1 + cross - 1)
+
+        @pl.when(has_left)
+        def _(chunk=chunk):
             leftward(chunk).start()
 
-    @pl.when(has_right)
-    def _():
-        for chunk in range(CHUNKS):
+        @pl.when(has_right)
+        def _(chunk=chunk):
             rightward(chunk).start()
+
+        if chunk == SEND_SUMS - 1:
+            send_sums()
 
     @pl.when(me == 0)
     def _():
@@ -212,35 +233,6 @@
     for index in range(COEFS):
         coef[index] = jnp.broadcast_to(turned[:, index : index + 1], (pencils, BLOCK))
     shift_of[...] = jnp.broadcast_to(turned[:, COEFS : COEFS + 1], (pencils, BLOCK)).astype(jnp.int32)
-
-    for copy in sum_copies:
-        copy.wait_recv()
-    before = jnp.zeros((8, pencils), jnp.float32)
-    whole = jnp.zeros((8, pencils), jnp.float32)
-    for index in range(chain):
-        value = sums[index]
-        before = before + jnp.where(index < me, value, 0.0)
-        whole = whole + value
-    parts[plane] = jnp.broadcast_to(jnp.sum(whole, axis=1, keepdims=True), (8, BLOCK))
-    part_copies = []
-    for step in range(1, cross):
-        copy = pltpu.make_async_remote_copy(
-            src_ref=parts.at[plane], dst_ref=parts.at[plane],
-            send_sem=part_send.at[step], recv_sem=part_recv.at[step],
-            device_id={"cross": lax.rem(plane + step, cross)}, device_id_type=MESH,
-        )
-        copy.start()
-        part_copies.append(copy)
-    raw[0:8, :] = before
-    turned = jnp.transpose(raw[...])
-    for var in range(VARS):
-        carried[var] = jnp.broadcast_to(turned[:, var : var + 1], (pencils, BLOCK))
-    for copy in part_copies:
-        copy.wait_recv()
-    grand = parts[0]
-    for index in range(1, cross):
-        grand = grand + parts[index]
-    mean_of[...] = grand / float(pencils * cross)
 
     source_cell = lax.broadcasted_iota(jnp.int32, (2 * BLOCK, BLOCK), 0)
     target_cell = lax.broadcasted_iota(jnp.int32, (2 * BLOCK, BLOCK), 1)
@@ -260,8 +252,52 @@
         value = jnp.where(ahead, values[0], values[1])
         return pltpu.roll(value, (-(STRIDE * row + SHIFT_MAX)) % BLOCK, 1)
 
+    part_copies = [
+        pltpu.make_async_remote_copy(
+            src_ref=parts.at[plane], dst_ref=parts.at[plane],
+            send_sem=part_send.at[step], recv_sem=part_recv.at[step],
+            device_id={"cross": lax.rem(plane + step, cross)}, device_id_type=MESH,
+        )
+        for step in range(1, cross)
+    ]
+
+    def reduce_chain():
+        for copy in sum_copies:
+            copy.wait_recv()
+        before = jnp.zeros((8, pencils), jnp.float32)
+        whole = jnp.zeros((8, pencils), jnp.float32)
+        for index in range(chain):
+            value = sums[index]
+            before = before + jnp.where(index < me, value, 0.0)
+            whole = whole + value
+        parts[plane] = jnp.broadcast_to(jnp.sum(whole, axis=1, keepdims=True), (8, BLOCK))
+        for copy in part_copies:
+            copy.start()
+        raw[0:8, :] = before
+        turned = jnp.transpose(raw[...])
+        for var in range(VARS):
+            carried[var] = jnp.broadcast_to(turned[:, var : var + 1], (pencils, BLOCK))
+
+    def finish_sums():
+        for copy in part_copies:
+            copy.wait_recv()
+        grand = parts[0]
+        for index in range(1, cross):
+            grand = grand + parts[index]
+        mean_of[...] = grand / float(pencils * cross)
+
+    def finish(var):
+        mass[var] = (mass[var] + carried[var]) / mean_of[var : var + 1, :]
+
     ready = 0
     for var in range(VARS):
+        if var == SUMS_AT:
+            reduce_chain()
+        if var == VARS - 1:
+            finish_sums()
+            for done in range(VARS - 1):
+                finish(done)
+
         needed = last_chunk(var) + 1
         if needed > ready:
             low, ready = ready, needed
@@ -316,14 +352,15 @@
             value = coef[2 * MOMENTS * MOMENTS, rows, :] * here[0]
             for m in range(1, MOMENTS):
                 value = value + coef[2 * MOMENTS * MOMENTS + m, rows, :] * here[m]
-            mass[var, rows, :] = value + carried[var, rows, :]
+            mass[var, rows, :] = value
             return carry
 
         lax.fori_loop(0, groups, remap, 0)
         summed = jnp.dot(
             window[...], triangle, precision=HIGHEST, preferred_element_type=jnp.float32
         )
-        mass[var] = (summed + mass[var]) / mean_of[var : var + 1, :]
+        mass[var] = summed + mass[var]
+    finish(VARS - 1)
 
     for copy in sum_copies + part_copies:
         copy.wait_send()
@@ -353,9 +390,13 @@
                 jax.ShapeDtypeStruct(moments.shape, jnp.float32),
                 jax.ShapeDtypeStruct((VARS, pencils, cells), jnp.float32),
             ),
-            in_specs=[pl.BlockSpec(memory_space=pltpu.VMEM)] * 4,
+            in_specs=[pl.BlockSpec(memory_space=pltpu.HBM)] * 4,
             out_specs=(pl.BlockSpec(memory_space=pltpu.VMEM),) * 2,
             scratch_shapes=[
+                pltpu.VMEM(moments.shape, jnp.float32),
+                pltpu.VMEM(flags.shape, jnp.int32),
+                pltpu.VMEM((1, pencils), jnp.int32),
+                pltpu.VMEM((1, pencils), jnp.float32),
                 chunk, chunk, chunk, chunk,
                 pltpu.VMEM((chain, 8, pencils), jnp.float32),
                 pltpu.VMEM((cross, 8, BLOCK), jnp.float32),
@@ -366,12 +407,15 @@
                 pltpu.VMEM((8, BLOCK), jnp.float32),
                 pltpu.VMEM((pencils, 2 * BLOCK), jnp.float32),
                 dma((CHUNKS,)), dma((CHUNKS,)), dma((CHUNKS,)), dma((CHUNKS,)),
-                dma((chain,)), dma((chain,)), dma((cross,)), dma((cross,)),
+                dma((chain,)), dma((chain,)), dma((cross,)), dma((cross,)), dma((4,)),
             ],
             compiler_params=pltpu.CompilerParams(
                 collective_id=0, has_side_effects=True, vmem_limit_bytes=48 << 20
             ),
-        )(moments, flags, shifts.T, fraction.reshape(1, pencils))
+        )(*(
+            pltpu.with_memory_space_constraint(value, pltpu.HBM)
+            for value in (moments, flags, shifts.T, fraction.reshape(1, pencils))
+        ))
 
     in_specs = (P(None, "cross", "chain"), P("cross", "chain"), P("cross", "chain"), P("cross"))
     out_specs = (P(None, "cross", "chain"), P(None, "cross", "chain"))

time: 34.2 us -> 22.7 us (0.66)
  the two profiles are of different devices: /device:TPU:0 before, /device:TPU:1 now
where the time goes in v2:
time: 22.7 us; the launch traced here: 22.6 us
  Pallas kernels  20.2 us (89%)
  local copies, waits for them, and re-layouts  1.78 us (8%)
  between operations  0.64 us (3%)
    pallas_call x1, Pallas kernels, shards(): pl.pallas_call(functools.partial(kernel, chain, cross), out_shape=(jax.Sh...  20.2 us
    unnamed x2, local copies, waits for them, and re-layouts  1.78 us

profile of v2, /device:TPU:1, one launch (start us, length us, event | category | flops | bytes accessed | tf_op | source)
XLA Modules:
  0.0 22.6 jit_solution(8803568681179823261)
XLA Ops:
  0.6 20.2 %shard_map.59 = (f32[20,128,128]{2,1,0:T(8,128)S(1)}, f32[5,128,128]{2,1,0:T(8,128)S(1)}) custom-call(f32[20,128,128]{2,1,0:T(8,128)} %moments_in.1, s32[128,128]{1,0:T(8,128)} %flags_in.1, s32[1,128]{1,0:T(1,128)} %bitcast.2, f32[1,128]{1,0:T(1,128)} %bitcast.3), custom_call_target="tpu_custom_call" | custom-call | tf_op jit(solution)/shard_map/pallas_call | solution.py:387
  20.8 1.1 %copy.8 = f32[20,128,128]{2,1,0:T(8,128)} copy(f32[20,128,128]{2,1,0:T(8,128)S(1)} %get-tuple-element.4) | data formatting | bytes 2621440
  21.9 0.7 %copy.9 = f32[5,128,128]{2,1,0:T(8,128)} copy(f32[5,128,128]{2,1,0:T(8,128)S(1)} %get-tuple-element.5) | data formatting | bytes 655360

commit v3 on v2

--- a/solution.py
+++ b/solution.py
@@ -1,6 +1,7 @@
 import functools
 
 import jax
+import numpy as np
 import jax.numpy as jnp
 from jax import lax
 from jax.experimental import pallas as pl
@@ -15,8 +16,9 @@
 STRIDE = SHIFT_MAX + 1
 CHUNKS = -(-ROWS * STRIDE // BLOCK)
 GROUP = 64
+RELAYED = tuple(range(1, CHUNKS, 2))
 SEND_SUMS = 2
-SUMS_AT = 3
+SUMS_AT = 2
 COEFS = 2 * MOMENTS * MOMENTS + MOMENTS
 MESH = pl.DeviceIdType.MESH
 HIGHEST = lax.Precision.HIGHEST
@@ -93,14 +95,34 @@
     ]
 
 
+def corner_relays(mesh):
+    ring = np.moveaxis(mesh.devices, mesh.axis_names.index("chain"), 0).reshape(mesh.shape["chain"], -1)[:, 0]
+    if any(getattr(device, "coords", None) is None for device in ring):
+        return {}, {}
+    spots = [tuple(device.coords) for device in ring]
+    rightward, leftward = {}, {}
+    if len({spot[0] for spot in spots}) == 2 and len({spot[1] for spot in spots}) == 2:
+        for index in range(len(spots) - 1):
+            low, high = spots[index], spots[index + 1]
+            if low[0] != high[0] and low[1] != high[1]:
+                for found, source, target, pick in (
+                    (rightward, index, index + 1, max), (leftward, index + 1, index, min)
+                ):
+                    corner = (spots[source][0], spots[target][1])
+                    at = [i for i, spot in enumerate(spots) if spot[:2] == corner]
+                    if at:
+                        found[source] = (pick(at), target)
+    return rightward, leftward
+
+
 def kernel(
-    chain, cross,
+    chain, cross, relays,
     moments_in, flags_in, shifts_in, fraction_in,
     remapped, mass,
     moments, flags, shifts, fraction,
     to_left, to_right, from_left, from_right,
     sums, parts, raw, coef, carried, shift_of, mean_of, window,
-    left_send, left_recv, right_send, right_recv,
+    relay, left_send, left_recv, right_send, right_recv, relay_send, relay_recv,
     sum_send, sum_recv, part_send, part_recv, input_sem,
 ):
     pencils = moments.shape[1]
@@ -198,18 +220,42 @@
 
         lax.fori_loop(0, groups, body, 0)
 
+    right_relays, left_relays = relays
+
+    def to_relay(chunk, source, send_sem, through):
+        return pltpu.make_async_remote_copy(
+            src_ref=source.at[chunk], dst_ref=relay.at[chunk],
+            send_sem=send_sem.at[chunk], recv_sem=relay_recv.at[chunk],
+            device_id={"chain": jnp.int32(through)}, device_id_type=MESH,
+        )
+
+    def onward(chunk, landing, recv_sem, target):
+        return pltpu.make_async_remote_copy(
+            src_ref=relay.at[chunk], dst_ref=landing.at[chunk],
+            send_sem=relay_send.at[chunk], recv_sem=recv_sem.at[chunk],
+            device_id={"chain": jnp.int32(target)}, device_id_type=MESH,
+        )
+
+    def send(chunk, direct, wanted, routes, source, send_sem):
+        if chunk in RELAYED:
+            for start, (through, _) in routes.items():
+                wanted = wanted & (me != start)
+
+                @pl.when(me == start)
+                def _():
+                    to_relay(chunk, source, send_sem, through).start()
+
+        @pl.when(wanted)
+        def _():
+            direct(chunk).start()
+
     for chunk in range(CHUNKS):
         pack(chunk)
         if chunk == 0:
             pl.semaphore_wait(barrier, chain - 1 + cross - 1)
 
-        @pl.when(has_left)
-        def _(chunk=chunk):
-            leftward(chunk).start()
-
-        @pl.when(has_right)
-        def _(chunk=chunk):
-            rightward(chunk).start()
+        send(chunk, leftward, has_left, left_relays, to_left, left_send)
+        send(chunk, rightward, has_right, right_relays, to_right, right_send)
 
         if chunk == SEND_SUMS - 1:
             send_sums()
@@ -260,6 +306,18 @@
         )
         for step in range(1, cross)
     ]
+
+    def pass_on(chunk):
+        for routes, source, send_sem, landing, recv_sem in (
+            (right_relays, to_right, right_send, from_left, right_recv),
+            (left_relays, to_left, left_send, from_right, left_recv),
+        ):
+            for through, target in routes.values():
+
+                @pl.when(me == through)
+                def _():
+                    to_relay(chunk, source, send_sem, through).wait_recv()
+                    onward(chunk, landing, recv_sem, target).start()
 
     def reduce_chain():
         for copy in sum_copies:
@@ -291,6 +349,8 @@
 
     ready = 0
     for var in range(VARS):
+        for chunk in RELAYED[var:] if var == VARS - 1 else RELAYED[var : var + 1]:
+            pass_on(chunk)
         if var == SUMS_AT:
             reduce_chain()
         if var == VARS - 1:
@@ -365,6 +425,16 @@
     for copy in sum_copies + part_copies:
         copy.wait_send()
 
+    for routes, landing, recv_sem in (
+        (right_relays, from_left, right_recv), (left_relays, from_right, left_recv)
+    ):
+        for through, target in routes.values():
+
+            @pl.when(me == through)
+            def _():
+                for chunk in RELAYED:
+                    onward(chunk, landing, recv_sem, target).wait_send()
+
     @pl.when(has_left)
     def _():
         for chunk in range(CHUNKS):
@@ -378,6 +448,7 @@
 
 def solution(mesh):
     chain, cross = mesh.shape["chain"], mesh.shape["cross"]
+    relays = corner_relays(mesh)
 
     def shards(moments, flags, shifts, fraction):
         row_count, pencils, cells = moments.shape
@@ -385,7 +456,7 @@
         chunk = pltpu.VMEM((CHUNKS, pencils, BLOCK), jnp.float32)
         dma = pltpu.SemaphoreType.DMA
         return pl.pallas_call(
-            functools.partial(kernel, chain, cross),
+            functools.partial(kernel, chain, cross, relays),
             out_shape=(
                 jax.ShapeDtypeStruct(moments.shape, jnp.float32),
                 jax.ShapeDtypeStruct((VARS, pencils, cells), jnp.float32),
@@ -406,7 +477,8 @@
                 pltpu.VMEM((pencils, BLOCK), jnp.int32),
                 pltpu.VMEM((8, BLOCK), jnp.float32),
                 pltpu.VMEM((pencils, 2 * BLOCK), jnp.float32),
-                dma((CHUNKS,)), dma((CHUNKS,)), dma((CHUNKS,)), dma((CHUNKS,)),
+                chunk, dma((CHUNKS,)), dma((CHUNKS,)), dma((CHUNKS,)), dma((CHUNKS,)),
+                dma((CHUNKS,)), dma((CHUNKS,)),
                 dma((chain,)), dma((chain,)), dma((cross,)), dma((cross,)), dma((4,)),
             ],
             compiler_params=pltpu.CompilerParams(

time: 22.7 us -> 21.2 us (0.934)
  the two profiles are of different devices: /device:TPU:1 before, /device:TPU:3 now
where the time goes in v3:
time: 21.2 us; the launch traced here: 21 us
  Pallas kernels  18.6 us (88%)
  local copies, waits for them, and re-layouts  1.78 us (8%)
  between operations  0.64 us (3%)
    pallas_call x1, Pallas kernels, shards(): pl.pallas_call(functools.partial(kernel, chain, cross, relays), out_shape...  18.6 us
    unnamed x2, local copies, waits for them, and re-layouts  1.78 us

profile of v3, /device:TPU:3, one launch (start us, length us, event | category | flops | bytes accessed | tf_op | source)
XLA Modules:
  0.0 21.0 jit_solution(15880406425406668440)
XLA Ops:
  0.6 18.6 %shard_map.59 = (f32[20,128,128]{2,1,0:T(8,128)S(1)}, f32[5,128,128]{2,1,0:T(8,128)S(1)}) custom-call(f32[20,128,128]{2,1,0:T(8,128)} %moments_in.1, s32[128,128]{1,0:T(8,128)} %flags_in.1, s32[1,128]{1,0:T(1,128)} %bitcast.2, f32[1,128]{1,0:T(1,128)} %bitcast.3), custom_call_target="tpu_custom_call" | custom-call | tf_op jit(solution)/shard_map/pallas_call | solution.py:458
  19.2 1.1 %copy.8 = f32[20,128,128]{2,1,0:T(8,128)} copy(f32[20,128,128]{2,1,0:T(8,128)S(1)} %get-tuple-element.4) | data formatting | bytes 2621440
  20.3 0.7 %copy.9 = f32[5,128,128]{2,1,0:T(8,128)} copy(f32[5,128,128]{2,1,0:T(8,128)S(1)} %get-tuple-element.5) | data formatting | bytes 655360

commit v4 on v3

--- a/solution.py
+++ b/solution.py
@@ -18,7 +18,7 @@
 GROUP = 64
 RELAYED = tuple(range(1, CHUNKS, 2))
 SEND_SUMS = 2
-SUMS_AT = 2
+SUMS_AT = 1
 COEFS = 2 * MOMENTS * MOMENTS + MOMENTS
 MESH = pl.DeviceIdType.MESH
 HIGHEST = lax.Precision.HIGHEST

time: 21.2 us -> 20.6 us (0.972)
  the two profiles are of different devices: /device:TPU:3 before, /device:TPU:1 now
where the time goes in v4:
time: 20.6 us; the launch traced here: 20.4 us
  Pallas kernels  18 us (87%)
  local copies, waits for them, and re-layouts  1.78 us (9%)
  between operations  0.64 us (3%)
    pallas_call x1, Pallas kernels, shards(): pl.pallas_call(functools.partial(kernel, chain, cross, relays), out_shape...  18 us
    unnamed x2, local copies, waits for them, and re-layouts  1.78 us

profile of v4, /device:TPU:1, one launch (start us, length us, event | category | flops | bytes accessed | tf_op | source)
XLA Modules:
  0.0 20.4 jit_solution(7331579957627673762)
XLA Ops:
  0.6 18.0 %shard_map.59 = (f32[20,128,128]{2,1,0:T(8,128)S(1)}, f32[5,128,128]{2,1,0:T(8,128)S(1)}) custom-call(f32[20,128,128]{2,1,0:T(8,128)} %moments_in.1, s32[128,128]{1,0:T(8,128)} %flags_in.1, s32[1,128]{1,0:T(1,128)} %bitcast.2, f32[1,128]{1,0:T(1,128)} %bitcast.3), custom_call_target="tpu_custom_call" | custom-call | tf_op jit(solution)/shard_map/pallas_call | solution.py:458
  18.6 1.1 %copy.8 = f32[20,128,128]{2,1,0:T(8,128)} copy(f32[20,128,128]{2,1,0:T(8,128)S(1)} %get-tuple-element.4) | data formatting | bytes 2621440
  19.7 0.7 %copy.9 = f32[5,128,128]{2,1,0:T(8,128)} copy(f32[5,128,128]{2,1,0:T(8,128)S(1)} %get-tuple-element.5) | data formatting | bytes 655360
